TPU v7x, 32 devices: a whole 2x2x4 slice. The times are simulated.
32 devices in a mesh: layer: 4 (over x, core), ex: 8 (over z, y).
Axes of the slice: x: 2, y: 2, z: 4, core: 2. Of those that a mesh axis runs over, the one named last changes fastest.
Arguments:
- queries: bfloat16 [128, 8, 4096], P('ex', 'layer'), may hold values from -6 to 6
- stored: bfloat16 [2048, 8, 4096], P('ex', 'layer'), may hold values from -0.03125 to 0.03125
- left_inv: bfloat16 [8, 64, 64], P('layer'), may hold values from -0.078125 to 2
- right_inv: bfloat16 [8, 64, 64], P('layer'), may hold values from -0.078125 to 2
Outputs:
- scores: float32 [128, 2048], P('layer', 'ex')
All inputs are finite; a program needn't handle non-finite values.
Results may differ from a plain program's by a relative error of at most 0.0041.
Values may be sent and summed in bfloat16 or wider, within the bound.
A program may use at most 128 MiB of HBM per device.

v0:
```python
import jax
import jax.numpy as jnp
from jax import lax
from jax.sharding import PartitionSpec as P


def precondition(gradients, left_inv, right_inv):
    count = gradients.shape[0]
    layers_here = gradients.shape[1]
    side = left_inv.shape[1]
    mats = gradients.reshape(count, layers_here, side, side)
    left_side = jnp.einsum(
        "lia,qlaj->qlij", left_inv, mats, preferred_element_type=jnp.float32
    ).astype(jnp.bfloat16)
    ready = jnp.einsum(
        "qlib,lbj->qlij", left_side, right_inv, preferred_element_type=jnp.float32
    ).astype(jnp.bfloat16)
    return ready.reshape(count, layers_here * side * side)


def shards(queries, stored, left_inv, right_inv):
    stored_flat = stored.reshape(stored.shape[0], stored.shape[1] * stored.shape[2])
    own_ready = precondition(queries, left_inv, right_inv)
    partial_value = lax.dot_general(
        lax.all_gather(own_ready, "ex", axis=0, tiled=True),
        stored_flat,
        (((1,), (1,)), ((), ())),
        preferred_element_type=jnp.float32,
    )
    return lax.psum_scatter(partial_value, "layer", scatter_dimension=0, tiled=True)


def solution(mesh):
    placed = (
        P("ex", "layer", None),
        P("ex", "layer", None),
        P("layer", None, None),
        P("layer", None, None),
    )
    return jax.shard_map(
        shards, mesh=mesh, in_specs=placed, out_specs=P("layer", "ex"), check_vma=False
    )
```

profile of v0, /device:TPU:0, one launch (start us, length us, event | category | flops | bytes accessed | tf_op | source)
XLA Modules:
  0.0 92.5 jit_solution(12882949968957154672)
XLA Ops:
  6.5 0.0 copy-start
  6.5 0.0 all-gather.2.cloned.1.call-start
  6.5 1.3 %reshape.9 = bf16[16,2,64,64]{3,2,1,0:T(8,128)(2,1)S(1)} reshape(bf16[16,2,4096]{2,1,0:T(2,128)(2,1)} %param.4) | data formatting | bytes 524288 | tf_op jit(solution)/shard_map/reshape | solution.py:11
  7.9 0.0 copy-done
  7.9 1.2 %fusion = bf16[16,2,64,64]{3,2,0,1:T(8,128)(2,1)S(1)} fusion(bf16[16,2,64,64]{3,2,1,0:T(8,128)(2,1)S(1)} %reshape.9, bf16[2,64,64]{2,1,0:T(8,128)(2,1)S(1)} %copy-done, bf16[2,64,64]{2,1,0:T(8,128)(2,1)} %param.6), kind=kOutput, calls=%fused_computation.2 | convolution fusion | flops 33816576 | bytes 557056 | tf_op jit(solution)/shard_map/qlib,lbj->qlij/dot_general | solution.py:15
  9.2 1.2 %reshape.10 = bf16[16,8192]{1,0:T(8,128)(2,1)} reshape(bf16[16,2,64,64]{3,2,1,0:T(8,128)(2,1)S(1)} %copy.5) | data formatting | bytes 524288 | tf_op jit(solution)/shard_map/reshape | solution.py:18
  10.3 0.0 all-gather.2.cloned.1.call-update
  10.4 0.0 reduce-scatter.2.cloned.1.call-start
  10.4 8.6 %copy.9 = bf16[32,8,2,4096]{3,1,2,0:T(8,128)(2,1)} copy(bf16[32,8,2,4096]{3,2,1,0:T(2,128)(2,1)} %bitcast.24) | data formatting | bytes 8388608
  19.0 43.3 %all-gather.2.cloned.1.call-done = bf16[128,8192]{1,0:T(8,128)(2,1)} async-done(((bf16[16,8192]{1,0:T(8,128)(2,1)}), bf16[128,8192]{1,0:T(8,128)(2,1)}) %all-gather.2.cloned.1.call-update) | async-done | bytes 2097168 | tf_op jit(solution)/shard_map/all_gather | solution.py:25
  62.3 5.0 %fusion.7 = f32[128,256]{1,0:T(8,128)} fusion(bf16[128,8192]{1,0:T(8,128)(2,1)} %all-gather.2.cloned.1.call-done, bf16[256,8192]{1,0:T(8,128)(2,1)} %bitcast.23), kind=kOutput, calls=%fused_computation.7 | convolution fusion | flops 536870912 | bytes 6422528 | tf_op jit(solution)/shard_map/dot_general | solution.py:24
  67.3 0.0 reduce-scatter.2.cloned.1.call-update
  67.4 18.3 %reduce-scatter.2.cloned.1.call-done = f32[32,256]{1,0:T(8,128)} async-done(((f32[128,256]{1,0:T(8,128)}), f32[32,256]{1,0:T(8,128)}) %reduce-scatter.2.cloned.1.call-update) | async-done | bytes 32784 | tf_op jit(solution)/shard_map/reduce_scatter | solution.py:30
  (1 shorter events, 0.0 us)
Async XLA Ops:
  6.5 1.4 %copy-start = (bf16[2,64,64]{2,1,0:T(8,128)(2,1)S(1)}, bf16[2,64,64]{2,1,0:T(8,128)(2,1)}, u32[]{:S(2)}) copy-start(bf16[2,64,64]{2,1,0:T(8,128)(2,1)} %param.7) | copy-start | bytes 49156
  6.5 55.8 %all-gather.2.cloned.1.call-start = ((), (), s32[]{:S(2)}) async-start(), calls=%async_computation.1 | async-start | bytes 2359296 | tf_op jit(solution)/shard_map/all_gather | solution.py:25
  10.4 75.3 %reduce-scatter.2.cloned.1.call-start = ((), (), s32[]{:S(2)}) async-start(), calls=%async_computation.2 | async-start | bytes 163840 | tf_op jit(solution)/shard_map/reduce_scatter | solution.py:30
Sparse Core Ops, SparseCore 0:
  10.5 51.7 all-gather.1
  67.5 18.1 reduce-scatter.1
where the time goes:
time: 92.8 us; the launch traced here: 92.5 us
  waiting for transfers between devices  61.6 us (66%)
  between operations  13.4 us (14%)
  local copies, waits for them, and re-layouts  11.2 us (12%)
  matrix products  6.23 us (7%)
    all_gather x1, waiting for transfers between devices, shards(): lax.all_gather(own_ready, 'ex', axis=0, tiled=True)  43.3 us
    reduce_scatter x1, waiting for transfers between devices, shards(): lax.psum_scatter(partial_value, 'layer', scatter_dimension=0, tiled=True)  18.3 us
    unnamed x3, local copies, waits for them, and re-layouts  8.62 us
    dot_general x1, matrix products, shards(): lax.dot_general(lax.all_gather(own_ready, 'ex', axis=0, tiled=True), stor...  5.01 us
  transfers between devices with their start and end apart: 2, of which 2 were waited for; matrix products, arithmetic and copies ran while one was open for 9% of the time, Pallas kernels for 0%

commit v1 on v0

--- a/solution.py
+++ b/solution.py
@@ -2,6 +2,12 @@
 import jax.numpy as jnp
 from jax import lax
 from jax.sharding import PartitionSpec as P
+
+
+def tiled_gather(x, axis, dim):
+    devices = lax.axis_size(axis)
+    repeats = [devices if d == dim else 1 for d in range(x.ndim)]
+    return lax.all_to_all(jnp.tile(x, repeats), axis, split_axis=dim, concat_axis=dim, tiled=True)
 
 
 def precondition(gradients, left_inv, right_inv):
@@ -22,7 +28,7 @@
     stored_flat = stored.reshape(stored.shape[0], stored.shape[1] * stored.shape[2])
     own_ready = precondition(queries, left_inv, right_inv)
     partial_value = lax.dot_general(
-        lax.all_gather(own_ready, "ex", axis=0, tiled=True),
+        tiled_gather(own_ready, "ex", 0),
         stored_flat,
         (((1,), (1,)), ((), ())),
         preferred_element_type=jnp.float32,

time: 92.8 us -> 97.1 us (1.046)
  starting transfers between devices: 0.04 us -> 7.35 us
  waiting for transfers between devices: 61.6 us -> 58.4 us
    all_gather x1 -> x0, waiting for transfers between devices: 43.3 us -> none  [shards(): lax.all_gather(own_ready, 'ex', axis=0, tiled=True)]
    all_to_all x0 -> x1, waiting for transfers between devices: none -> 39.6 us  [tiled_gather(): lax.all_to_all(jnp.tile(x, repeats), axis, split_axis=dim, concat_axis=di...]
    all_to_all x0 -> x1, starting transfers between devices: none -> 7.31 us  [tiled_gather(): lax.all_to_all(jnp.tile(x, repeats), axis, split_axis=dim, concat_axis=di...]
    another operation x0 -> x2, local copies, waits for them, and re-layouts: none -> 1.98 us  [tiled_gather(): jnp.tile(x, repeats)]
    reshape x1 -> x0, local copies, waits for them, and re-layouts: 1.18 us -> none  [precondition(): return ready.reshape(count, layers_here * side * side)]
where the time goes in v1:
time: 97.1 us; the launch traced here: 96.8 us
  waiting for transfers between devices  58.4 us (60%)
  between operations  13.4 us (14%)
  local copies, waits for them, and re-layouts  12 us (12%)
  starting transfers between devices  7.35 us (8%)
  matrix products  5.59 us (6%)
    all_to_all x1, waiting for transfers between devices, tiled_gather(): lax.all_to_all(jnp.tile(x, repeats), axis, split_axis=dim, concat_axis=di...  39.6 us
    reduce_scatter x1, waiting for transfers between devices, shards(): lax.psum_scatter(partial_value, 'layer', scatter_dimension=0, tiled=True)  18.9 us
    unnamed x3, local copies, waits for them, and re-layouts  8.62 us
    all_to_all x1, starting transfers between devices, tiled_gather(): lax.all_to_all(jnp.tile(x, repeats), axis, split_axis=dim, concat_axis=di...  7.31 us
    dot_general x1, matrix products, shards(): lax.dot_general(tiled_gather(own_ready, 'ex', 0), stored_flat, (((1,), (1...  4.37 us
    another operation x2, local copies, waits for them, and re-layouts, tiled_gather(): jnp.tile(x, repeats)  1.98 us
  transfers between devices with their start and end apart: 2, of which 2 were waited for; matrix products, arithmetic and copies ran while one was open for 9% of the time, Pallas kernels for 0%

profile of v1, /device:TPU:0, one launch (start us, length us, event | category | flops | bytes accessed | tf_op | source)
XLA Modules:
  0.0 96.8 jit_solution(8803114477664471187)
XLA Ops:
  6.5 0.0 copy-start
  6.5 1.3 %reshape.13 = bf16[16,2,64,64]{3,2,1,0:T(8,128)(2,1)S(1)} reshape(bf16[16,2,4096]{2,1,0:T(2,128)(2,1)} %param.4) | data formatting | bytes 524288 | tf_op jit(solution)/shard_map/reshape | solution.py:17
  7.9 0.0 copy-done
  7.9 1.2 %fusion = bf16[16,2,64,64]{3,2,0,1:T(8,128)(2,1)S(1)} fusion(bf16[16,2,64,64]{3,2,1,0:T(8,128)(2,1)S(1)} %reshape.13, bf16[2,64,64]{2,1,0:T(8,128)(2,1)S(1)} %copy-done, bf16[2,64,64]{2,1,0:T(8,128)(2,1)} %param.6), kind=kOutput, calls=%fused_computation.2 | convolution fusion | flops 33816576 | bytes 557056 | tf_op jit(solution)/shard_map/qlib,lbj->qlij/dot_general | solution.py:21
  9.2 0.5 tile.8
  9.6 1.5 %tile.9 = bf16[8,16,8192]{2,1,0:T(8,128)(2,1)} broadcast(bf16[16,8192]{1,0:T(8,128)(2,1)S(1)} %tile.8), dimensions={1,2} | broadcast | bytes 2359296 | tf_op jit(solution)/shard_map/tile | solution.py:10
  11.1 7.3 %all-to-all-start = ((bf16[8,16,8192]{2,1,0:T(8,128)(2,1)}), bf16[8,16,8192]{2,1,0:T(8,128)(2,1)S(1)}, u32[]{:S(2)}, u32[]{:S(2)}) async-start(bf16[8,16,8192]{2,1,0:T(8,128)(2,1)} %tile.9), calls=%async_computation | async-start | bytes 4194304 | tf_op jit(solution)/shard_map/all_to_all | solution.py:10
  18.5 0.0 reduce-scatter.2.cloned.1.call-start
  18.5 8.6 %copy.9 = bf16[32,8,2,4096]{3,1,2,0:T(8,128)(2,1)} copy(bf16[32,8,2,4096]{3,2,1,0:T(2,128)(2,1)} %bitcast.26) | data formatting | bytes 8388608
  27.1 39.6 %all-to-all-done = bf16[8,16,8192]{2,1,0:T(8,128)(2,1)S(1)} async-done(((bf16[8,16,8192]{2,1,0:T(8,128)(2,1)}), bf16[8,16,8192]{2,1,0:T(8,128)(2,1)S(1)}, u32[]{:S(2)}, u32[]{:S(2)}) %all-to-all-start) | async-done | bytes 2097184 | tf_op jit(solution)/shard_map/all_to_all | solution.py:10
  66.7 4.4 %fusion.7 = f32[128,256]{1,0:T(8,128)} fusion(bf16[128,8192]{1,0:T(8,128)(2,1)S(1)} %bitcast.25, bf16[256,8192]{1,0:T(8,128)(2,1)} %bitcast.24), kind=kOutput, calls=%fused_computation.7 | convolution fusion | flops 536870912 | bytes 6422528 | tf_op jit(solution)/shard_map/dot_general | solution.py:30
  71.1 0.0 reduce-scatter.2.cloned.1.call-update
  71.1 18.9 %reduce-scatter.2.cloned.1.call-done = f32[32,256]{1,0:T(8,128)} async-done(((f32[128,256]{1,0:T(8,128)}), f32[32,256]{1,0:T(8,128)}) %reduce-scatter.2.cloned.1.call-update) | async-done | bytes 32784 | tf_op jit(solution)/shard_map/reduce_scatter | solution.py:36
  (1 shorter events, 0.0 us)
Async XLA Ops:
  6.5 1.3 %copy-start = (bf16[2,64,64]{2,1,0:T(8,128)(2,1)S(1)}, bf16[2,64,64]{2,1,0:T(8,128)(2,1)}, u32[]{:S(2)}) copy-start(bf16[2,64,64]{2,1,0:T(8,128)(2,1)} %param.7) | copy-start | bytes 49156
  11.1 55.5 %all-to-all-start = ((bf16[8,16,8192]{2,1,0:T(8,128)(2,1)}), bf16[8,16,8192]{2,1,0:T(8,128)(2,1)S(1)}, u32[]{:S(2)}, u32[]{:S(2)}) async-start(bf16[8,16,8192]{2,1,0:T(8,128)(2,1)} %tile.9), calls=%async_computation | async-start | bytes 4194304 | tf_op jit(solution)/shard_map/all_to_all | solution.py:10
  18.5 71.5 %reduce-scatter.2.cloned.1.call-start = ((), (), s32[]{:S(2)}) async-start(), calls=%async_computation.2 | async-start | bytes 163840 | tf_op jit(solution)/shard_map/reduce_scatter | solution.py:36
Sparse Core Ops, SparseCore 0:
  71.2 18.6 reduce-scatter.1
